TPU v7x, 32 devices: a whole 2x2x4 slice. The times are simulated.
32 devices in a mesh: view: 4 (over y, core), row: 8 (over z, x).
Axes of the slice: x: 2, y: 2, z: 4, core: 2. Of those that a mesh axis runs over, the one named last changes fastest.
Arguments:
- features: float32 [4, 16384, 2048], P('view', 'row'), may hold values from -0.125 to 0.125
- view_maps: float32 [4, 2048, 256], P('view', 'row'), may hold values from -6 to 6
- shared: float32 [16384, 256], P('row'), may hold values from -6 to 6
Outputs:
- maps_out: float32 [4, 2048, 256], P('view', 'row')
- shared_out: float32 [16384, 256], P('row')
All inputs are finite; a program needn't handle non-finite values.
Results may differ from a plain program's by a relative error of at most 0.00013.
Values sent between devices are 32-bit elements; how exact they have to be, the bound alone decides.
A program may use at most 128 MiB of HBM per device.

v0:
```python
import jax
import jax.numpy as jnp
from jax import lax
from jax.sharding import PartitionSpec as P

ITERS = 2
NEWTON = 5
step_rate = 0.5


def newton_root(gram_matrix):
    highest = lax.Precision.HIGHEST
    frob_norm = jnp.sqrt(jnp.sum(gram_matrix * gram_matrix))
    scaled = gram_matrix / frob_norm
    identity = jnp.eye(gram_matrix.shape[0], dtype=jnp.float32)
    inverse_root = identity
    for newton_step in range(NEWTON):
        correction = 1.5 * identity - 0.5 * jnp.dot(inverse_root, scaled, precision=highest)
        scaled = jnp.dot(scaled, correction, precision=highest)
        inverse_root = jnp.dot(correction, inverse_root, precision=highest)
    return (inverse_root, frob_norm)


def local(features, view_maps, shared):
    highest = lax.Precision.HIGHEST
    samples = features[0]
    map_shard = view_maps[0]
    local_rows = samples.shape[0]
    width = samples.shape[1]
    shard_rows = map_shard.shape[0]
    total_rows = local_rows * lax.axis_size("row")
    view_count = lax.axis_size("view")
    step_size = step_rate * width / total_rows
    whole_map = lax.all_gather(map_shard, "row", axis=0, tiled=True)
    projected = jnp.dot(samples, whole_map, precision=highest)
    for iteration in range(ITERS):
        residual = projected - shared
        gradient = lax.psum(jnp.dot(samples.T, residual, precision=highest), "row")
        whole_map = whole_map - step_size * gradient
        projected = jnp.dot(samples, whole_map, precision=highest)
        average = lax.psum(projected, "view") / view_count
        gram_matrix = lax.psum(jnp.dot(average.T, average, precision=highest), "row")
        inverse_root, frob_norm = newton_root(gram_matrix)
        shared = jnp.dot(average, inverse_root, precision=highest) * jnp.sqrt(
            total_rows / frob_norm
        )
    map_shard = lax.dynamic_slice_in_dim(
        whole_map, lax.axis_index("row") * shard_rows, shard_rows, 0
    )
    return (map_shard[None], shared)


def solution(mesh):
    in_specs = (P("view", "row", None), P("view", "row", None), P("row", None))
    out_specs = (P("view", "row", None), P("row", None))
    return jax.shard_map(local, mesh=mesh, in_specs=in_specs, out_specs=out_specs, check_vma=False)
```

profile of v0, /device:TPU:0, one launch (start us, length us, event | category | flops | bytes accessed | tf_op | source)
XLA Modules:
  0.0 663.0 jit_solution(7803501747945105830)
XLA Ops:
  7.2 1.8 copy.6
  9.1 54.6 %all-gather.3.cloned.1.call-done = f32[1,2048,256]{1,2,0:T(8,128)} async-done(((f32[1,256,256]{1,2,0:T(8,128)}), f32[1,2048,256]{1,2,0:T(8,128)}) %all-gather.3.cloned.1.call-update) | async-done | bytes 2097168 | tf_op jit(solution)/shard_map/all_gather | solution.py:34
  63.7 17.4 %fusion.23 = f32[2048,256]{1,0:T(8,128)S(1)} fusion(f32[2048,256]{1,0:T(8,128)} %param.5, f32[1,2048,2048]{2,1,0:T(8,128)} %param.3, f32[1,2048,256]{1,2,0:T(8,128)} %all-gather.3.cloned.1.call-done), kind=kOutput, calls=%fused_computation.17 | convolution fusion | flops 12885426176 | bytes 23068672 | tf_op jit(solution)/shard_map/dot_general | solution.py:35
  81.1 31.3 %fusion.10 = f32[2048,256]{0,1:T(8,128)} fusion(f32[2048,256]{1,0:T(8,128)S(1)} %fusion.23, f32[1,2048,2048]{2,1,0:T(8,128)S(1)} %copy-done), kind=kOutput, calls=%fused_computation.10 | convolution fusion | flops 12884901888 | bytes 20971520 | tf_op jit(solution)/shard_map/dot_general | solution.py:38
  112.5 100.6 %all-reduce.7.cloned.1.call-done = f32[2048,256]{0,1:T(8,128)} async-done(((f32[2048,256]{0,1:T(8,128)}), f32[2048,256]{0,1:T(8,128)}) %all-reduce.7.cloned.1.call-update) | async-done | bytes 2097168 | tf_op jit(solution)/shard_map/psum | solution.py:38
  213.1 18.8 %fusion.13 = f32[2048,256]{0,1:T(8,128)} fusion(f32[1,2048,2048]{2,1,0:T(8,128)} %param.3, f32[1,2048,256]{1,2,0:T(8,128)S(1)} %copy-done.1, f32[2048,256]{0,1:T(8,128)} %all-reduce.7.cloned.1.call-done), kind=kOutput, calls=%fused_computation.11 | convolution fusion | flops 12885950464 | bytes 23068672 | tf_op jit(solution)/shard_map/dot_general | solution.py:40
  232.0 50.8 %all-reduce.9.cloned.1.call-done = f32[2048,256]{0,1:T(8,128)} async-done(((f32[2048,256]{0,1:T(8,128)}), f32[2048,256]{0,1:T(8,128)}) %all-reduce.9.cloned.1.call-update) | async-done | bytes 2097168 | tf_op jit(solution)/shard_map/psum | solution.py:41
  282.8 4.9 fusion.31
  287.7 71.2 %all-reduce.11.cloned.1.call-done = f32[256,256]{1,0:T(8,128)} async-done(((f32[256,256]{1,0:T(8,128)}), f32[256,256]{1,0:T(8,128)}) %all-reduce.11.cloned.1.call-update) | async-done | bytes 262160 | tf_op jit(solution)/shard_map/psum | solution.py:42
  358.9 1.6 multiply_reduce_fusion.1
  361.3 1.3 fusion.42
  362.8 1.3 fusion.49
  364.2 0.4 fusion.41
  364.5 0.4 fusion.57
  364.9 0.4 fusion.56
  365.3 0.4 fusion.40
  365.7 0.4 fusion.59
  366.1 0.4 fusion.58
  366.5 0.4 fusion.39
  366.9 0.4 fusion.61
  367.3 0.4 fusion.60
  367.6 0.4 fusion.38
  368.0 0.4 fusion.62
  368.5 4.4 fusion.22
  372.9 17.8 %fusion.16 = f32[2048,256]{0,1:T(8,128)} fusion(f32[2048,256]{0,1:T(8,128)S(1)} %fusion.22, f32[1,2048,2048]{2,1,0:T(8,128)} %param.3), kind=kOutput, calls=%fused_computation.12 | convolution fusion | flops 12884901888 | bytes 20971520 | tf_op jit(solution)/shard_map/dot_general | solution.py:38
  390.7 101.6 %all-reduce.13.cloned.1.call-done = f32[2048,256]{0,1:T(8,128)} async-done(((f32[2048,256]{0,1:T(8,128)}), f32[2048,256]{0,1:T(8,128)}) %all-reduce.13.cloned.1.call-update) | async-done | bytes 2097168 | tf_op jit(solution)/shard_map/psum | solution.py:38
  492.4 2.8 multiply_subtract_fusion
  495.2 1.3 copy-done.2
  496.5 17.9 %fusion.19 = f32[2048,256]{0,1:T(8,128)} fusion(f32[2048,256]{0,1:T(8,128)S(1)} %multiply_subtract_fusion, f32[1,2048,2048]{2,1,0:T(8,128)} %param.3), kind=kOutput, calls=%fused_computation.13 | convolution fusion | flops 12884901888 | bytes 20971520 | tf_op jit(solution)/shard_map/dot_general | solution.py:40
  514.7 50.6 %all-reduce.15.cloned.1.call-done = f32[2048,256]{0,1:T(8,128)} async-done(((f32[2048,256]{0,1:T(8,128)}), f32[2048,256]{0,1:T(8,128)}) %all-reduce.15.cloned.1.call-update) | async-done | bytes 2097168 | tf_op jit(solution)/shard_map/psum | solution.py:41
  565.2 4.9 fusion.28
  570.1 1.0 constant_dynamic-slice_fusion
  571.1 0.8 copy.7
  572.0 69.4 %all-reduce.17.cloned.1.call-done = f32[256,256]{1,0:T(8,128)} async-done(((f32[256,256]{1,0:T(8,128)}), f32[256,256]{1,0:T(8,128)}) %all-reduce.17.cloned.1.call-update) | async-done | bytes 262160 | tf_op jit(solution)/shard_map/psum | solution.py:42
  641.4 1.6 multiply_reduce_fusion
  643.7 1.3 fusion.37
  645.3 1.3 fusion.50
  646.6 0.4 fusion.36
  647.4 0.4 fusion.63
  647.8 0.4 fusion.35
  648.2 0.4 fusion.66
  648.6 0.4 fusion.65
  649.0 0.4 fusion.34
  649.3 0.4 fusion.68
  649.7 0.4 fusion.67
  650.2 0.4 fusion.33
  650.5 0.4 fusion.69
  651.0 4.8 convolution_multiply_fusion
  (24 shorter events, 1.6 us)
Async XLA Ops:
  7.2 56.5 %all-gather.3.cloned.1.call-start = ((), (), s32[]{:S(2)}) async-start(), calls=%async_computation.6 | async-start | bytes 2359296 | tf_op jit(solution)/shard_map/all_gather | solution.py:34
  9.0 204.1 %all-reduce.7.cloned.1.call-start = ((), (), s32[]{:S(2)}) async-start(), calls=%async_computation | async-start | bytes 4194304 | tf_op jit(solution)/shard_map/psum | solution.py:38
  63.7 17.4 %copy-start = (f32[1,2048,2048]{2,1,0:T(8,128)S(1)}, f32[1,2048,2048]{2,1,0:T(8,128)}, u32[]{:S(2)}) copy-start(f32[1,2048,2048]{2,1,0:T(8,128)} %param.3) | copy-start | bytes 50331652
  112.4 100.7 %copy-start.1 = (f32[1,2048,256]{1,2,0:T(8,128)S(1)}, f32[1,2048,256]{1,2,0:T(8,128)}, u32[]{:S(2)}) copy-start(f32[1,2048,256]{1,2,0:T(8,128)} %all-gather.3.cloned.1.call-done) | copy-start | bytes 6291460
  112.4 170.4 %all-reduce.9.cloned.1.call-start = ((), (), s32[]{:S(2)}) async-start(), calls=%async_computation.1 | async-start | bytes 4194304 | tf_op jit(solution)/shard_map/psum | solution.py:41
  231.9 127.0 %all-reduce.11.cloned.1.call-start = ((), (), s32[]{:S(2)}) async-start(), calls=%async_computation.2 | async-start | bytes 524288 | tf_op jit(solution)/shard_map/psum | solution.py:42
  287.7 204.7 %all-reduce.13.cloned.1.call-start = ((), (), s32[]{:S(2)}) async-start(), calls=%async_computation.3 | async-start | bytes 4194304 | tf_op jit(solution)/shard_map/psum | solution.py:38
  390.7 174.6 %all-reduce.15.cloned.1.call-start = ((), (), s32[]{:S(2)}) async-start(), calls=%async_computation.4 | async-start | bytes 4194304 | tf_op jit(solution)/shard_map/psum | solution.py:41
  495.2 1.3 copy-start.2
  514.4 127.0 %all-reduce.17.cloned.1.call-start = ((), (), s32[]{:S(2)}) async-start(), calls=%async_computation.5 | async-start | bytes 524288 | tf_op jit(solution)/shard_map/psum | solution.py:42
  648.9 2.0 copy-start.3
Sparse Core Ops, SparseCore 0:
  10.6 53.0 all-gather.2
  112.5 100.5 all-reduce.6
  232.1 50.6 all-reduce.8
  287.8 71.0 all-reduce.10
  390.8 101.5 all-reduce.12
  514.5 50.6 all-reduce.14
  570.3 71.0 all-reduce.16
where the time goes:
time: 667 us; the launch traced here: 663 us
  waiting for transfers between devices  499 us (75%)
  matrix products  136 us (20%)
  between operations  16.4 us (2%)
    psum x2, waiting for transfers between devices, local(): gradient = lax.psum(jnp.dot(samples.T, residual, precision=highest), 'row')  202 us
    psum x2, waiting for transfers between devices, local(): lax.psum(jnp.dot(average.T, average, precision=highest), 'row')  141 us
    psum x2, waiting for transfers between devices, local(): average = lax.psum(projected, 'view') / view_count  101 us
    all_gather x1, waiting for transfers between devices, local(): whole_map = lax.all_gather(map_shard, 'row', axis=0, tiled=True)  54.6 us
    dot_general x3, matrix products, local(): projected = jnp.dot(samples, whole_map, precision=highest)  54.1 us
    dot_general x2, matrix products, local(): gradient = lax.psum(jnp.dot(samples.T, residual, precision=highest), 'row')  49.1 us
  transfers between devices with their start and end apart: 7, of which 7 were waited for; matrix products, arithmetic and copies ran while one was open for 0% of the time, Pallas kernels for 0%

commit v1 on v0

--- a/solution.py
+++ b/solution.py
@@ -6,6 +6,11 @@
 ITERS = 2
 NEWTON = 5
 step_rate = 0.5
+
+
+def gather_from_all(array, axis, dim):
+    copies = jnp.concatenate([array] * lax.axis_size(axis), axis=dim)
+    return lax.all_to_all(copies, axis, dim, dim, tiled=True)
 
 
 def newton_root(gram_matrix):
@@ -31,7 +36,7 @@
     total_rows = local_rows * lax.axis_size("row")
     view_count = lax.axis_size("view")
     step_size = step_rate * width / total_rows
-    whole_map = lax.all_gather(map_shard, "row", axis=0, tiled=True)
+    whole_map = gather_from_all(map_shard, "row", 0)
     projected = jnp.dot(samples, whole_map, precision=highest)
     for iteration in range(ITERS):
         residual = projected - shared

time: 667 us -> 663 us (level)
  matrix products: 136 us -> 120 us
  local copies, waits for them, and re-layouts: 4.92 us -> 15.3 us
  waiting for transfers between devices: 499 us -> 490 us
  starting transfers between devices: 0.5 us -> 8.38 us
    all_gather x1 -> x0, waiting for transfers between devices: 54.6 us -> none  [local(): whole_map = lax.all_gather(map_shard, 'row', axis=0, tiled=True)]
    all_to_all x0 -> x1, waiting for transfers between devices: none -> 45.3 us  [gather_from_all(): return lax.all_to_all(copies, axis, dim, dim, tiled=True)]
    dot_general x2, matrix products: 49.1 us -> 33.4 us  [local(): gradient = lax.psum(jnp.dot(samples.T, residual, precision=highest), 'row')]
    all_to_all x0 -> x1, starting transfers between devices: none -> 7.28 us  [gather_from_all(): return lax.all_to_all(copies, axis, dim, dim, tiled=True)]
  transfers between devices with their start and end apart: 7 -> 7, of which waited for: 7 -> 7; matrix products, arithmetic and copies ran while one was open for 0% -> 1% of each run, Pallas kernels for 0% -> 0%
where the time goes in v1:
time: 663 us; the launch traced here: 656 us
  waiting for transfers between devices  490 us (74%)
  matrix products  120 us (18%)
  between operations  16.3 us (2%)
  local copies, waits for them, and re-layouts  15.3 us (2%)
  starting transfers between devices  8.38 us (1%)
    psum x2, waiting for transfers between devices, local(): gradient = lax.psum(jnp.dot(samples.T, residual, precision=highest), 'row')  202 us
    psum x2, waiting for transfers between devices, local(): lax.psum(jnp.dot(average.T, average, precision=highest), 'row')  140 us
    psum x2, waiting for transfers between devices, local(): average = lax.psum(projected, 'view') / view_count  102 us
    dot_general x3, matrix products, local(): projected = jnp.dot(samples, whole_map, precision=highest)  54 us
    all_to_all x1, waiting for transfers between devices, gather_from_all(): return lax.all_to_all(copies, axis, dim, dim, tiled=True)  45.3 us
    dot_general x2, matrix products, local(): gradient = lax.psum(jnp.dot(samples.T, residual, precision=highest), 'row')  33.4 us
  transfers between devices with their start and end apart: 7, of which 7 were waited for; matrix products, arithmetic and copies ran while one was open for 1% of the time, Pallas kernels for 0%

profile of v1, /device:TPU:0, one launch (start us, length us, event | category | flops | bytes accessed | tf_op | source)
XLA Modules:
  0.0 656.2 jit_solution(5307656627167751612)
XLA Ops:
  7.2 1.0 bitcast_dynamic-update-slice_fusion.6
  8.2 1.0 bitcast_dynamic-update-slice_fusion.5
  9.2 1.0 bitcast_dynamic-update-slice_fusion.4
  10.2 1.0 bitcast_dynamic-update-slice_fusion.3
  11.3 1.8 copy.12
  13.1 7.3 %all-to-all-start = ((f32[8,256,256]{1,2,0:T(8,128)}), f32[8,256,256]{1,2,0:T(8,128)S(1)}, u32[]{:S(2)}, u32[]{:S(2)}) async-start(f32[8,256,256]{1,2,0:T(8,128)} %copy.12), calls=%async_computation | async-start | bytes 4194304 | tf_op jit(solution)/shard_map/all_to_all | solution.py:13
  20.4 2.9 copy.14
  23.3 45.3 %all-to-all-done = f32[8,256,256]{1,2,0:T(8,128)S(1)} async-done(((f32[8,256,256]{1,2,0:T(8,128)}), f32[8,256,256]{1,2,0:T(8,128)S(1)}, u32[]{:S(2)}, u32[]{:S(2)}) %all-to-all-start) | async-done | bytes 2097184 | tf_op jit(solution)/shard_map/all_to_all | solution.py:13
  68.6 1.3 copy-done.3
  69.9 2.0 copy.18
  72.0 17.3 %fusion.26 = f32[2048,256]{0,1:T(8,128)S(1)} fusion(f32[2048,256]{0,1:T(8,128)} %copy.14, f32[2048,256]{0,1:T(8,128)S(1)} %bitcast.104, f32[1,2048,2048]{2,1,0:T(8,128)} %param.3), kind=kOutput, calls=%fused_computation.18 | convolution fusion | flops 12885426176 | bytes 23068672 | tf_op jit(solution)/shard_map/dot_general | solution.py:40
  89.3 15.6 %fusion.13 = f32[2048,256]{0,1:T(8,128)} fusion(f32[2048,256]{0,1:T(8,128)S(1)} %fusion.26, f32[1,2048,2048]{2,1,0:T(8,128)S(1)} %bitcast.103), kind=kOutput, calls=%fused_computation.11 | convolution fusion | flops 12884901888 | bytes 20971520 | tf_op jit(solution)/shard_map/dot_general | solution.py:43
  104.9 0.5 all-reduce.9.cloned.1.call-start
  105.4 101.0 %all-reduce.7.cloned.1.call-done = f32[2048,256]{0,1:T(8,128)} async-done(((f32[2048,256]{0,1:T(8,128)}), f32[2048,256]{0,1:T(8,128)}) %all-reduce.7.cloned.1.call-update) | async-done | bytes 2097168 | tf_op jit(solution)/shard_map/psum | solution.py:43
  206.5 18.8 %fusion.16 = f32[2048,256]{0,1:T(8,128)} fusion(f32[1,2048,2048]{2,1,0:T(8,128)} %param.3, f32[2048,256]{0,1:T(8,128)S(1)} %bitcast.105, f32[2048,256]{0,1:T(8,128)} %all-reduce.7.cloned.1.call-done), kind=kOutput, calls=%fused_computation.12 | convolution fusion | flops 12885950464 | bytes 23068672 | tf_op jit(solution)/shard_map/dot_general | solution.py:45
  225.4 50.8 %all-reduce.9.cloned.1.call-done = f32[2048,256]{0,1:T(8,128)} async-done(((f32[2048,256]{0,1:T(8,128)}), f32[2048,256]{0,1:T(8,128)}) %all-reduce.9.cloned.1.call-update) | async-done | bytes 2097168 | tf_op jit(solution)/shard_map/psum | solution.py:46
  276.2 4.9 fusion.33
  281.3 71.0 %all-reduce.11.cloned.1.call-done = f32[256,256]{1,0:T(8,128)} async-done(((f32[256,256]{1,0:T(8,128)}), f32[256,256]{1,0:T(8,128)}) %all-reduce.11.cloned.1.call-update) | async-done | bytes 262160 | tf_op jit(solution)/shard_map/psum | solution.py:47
  352.3 1.6 multiply_reduce_fusion.1
  354.6 1.3 fusion.44
  356.2 1.3 fusion.51
  357.5 0.4 fusion.43
  358.7 0.4 fusion.42
  359.9 0.4 fusion.41
  360.3 0.4 fusion.63
  360.6 0.4 fusion.62
  361.0 0.4 fusion.40
  361.9 4.3 fusion.25
  366.3 17.8 %fusion.19 = f32[2048,256]{0,1:T(8,128)} fusion(f32[2048,256]{0,1:T(8,128)S(1)} %fusion.25, f32[1,2048,2048]{2,1,0:T(8,128)} %param.3), kind=kOutput, calls=%fused_computation.13 | convolution fusion | flops 12884901888 | bytes 20971520 | tf_op jit(solution)/shard_map/dot_general | solution.py:43
  384.3 101.4 %all-reduce.13.cloned.1.call-done = f32[2048,256]{0,1:T(8,128)} async-done(((f32[2048,256]{0,1:T(8,128)}), f32[2048,256]{0,1:T(8,128)}) %all-reduce.13.cloned.1.call-update) | async-done | bytes 2097168 | tf_op jit(solution)/shard_map/psum | solution.py:43
  485.7 2.8 multiply_subtract_fusion
  488.6 1.3 copy-done.1
  489.9 17.8 %fusion.22 = f32[2048,256]{0,1:T(8,128)} fusion(f32[2048,256]{0,1:T(8,128)S(1)} %multiply_subtract_fusion, f32[1,2048,2048]{2,1,0:T(8,128)} %param.3), kind=kOutput, calls=%fused_computation.14 | convolution fusion | flops 12884901888 | bytes 20971520 | tf_op jit(solution)/shard_map/dot_general | solution.py:45
  507.8 50.8 %all-reduce.15.cloned.1.call-done = f32[2048,256]{0,1:T(8,128)} async-done(((f32[2048,256]{0,1:T(8,128)}), f32[2048,256]{0,1:T(8,128)}) %all-reduce.15.cloned.1.call-update) | async-done | bytes 2097168 | tf_op jit(solution)/shard_map/psum | solution.py:46
  558.6 4.9 fusion.30
  563.5 1.0 constant_dynamic-slice_fusion
  564.5 0.8 copy.16
  565.3 69.4 %all-reduce.17.cloned.1.call-done = f32[256,256]{1,0:T(8,128)} async-done(((f32[256,256]{1,0:T(8,128)}), f32[256,256]{1,0:T(8,128)}) %all-reduce.17.cloned.1.call-update) | async-done | bytes 262160 | tf_op jit(solution)/shard_map/psum | solution.py:47
  634.8 1.6 multiply_reduce_fusion
  637.1 1.3 fusion.39
  638.6 1.3 fusion.52
  640.0 0.4 fusion.38
  640.7 0.4 fusion.65
  641.1 0.4 fusion.37
  642.3 0.4 fusion.36
  643.1 0.4 fusion.69
  643.5 0.4 fusion.35
  644.3 4.8 convolution_multiply_fusion
  (42 shorter events, 5.1 us)
Async XLA Ops:
  7.2 4.0 copy-start
  13.1 55.5 %all-to-all-start = ((f32[8,256,256]{1,2,0:T(8,128)}), f32[8,256,256]{1,2,0:T(8,128)S(1)}, u32[]{:S(2)}, u32[]{:S(2)}) async-start(f32[8,256,256]{1,2,0:T(8,128)} %copy.12), calls=%async_computation | async-start | bytes 4194304 | tf_op jit(solution)/shard_map/all_to_all | solution.py:13
  20.3 186.1 %all-reduce.7.cloned.1.call-start = ((), (), s32[]{:S(2)}) async-start(), calls=%async_computation.1 | async-start | bytes 4194304 | tf_op jit(solution)/shard_map/psum | solution.py:43
  68.6 1.3 copy-start.3
  69.9 19.4 %slice-start = ((s8[16777216]{0:T(1024)(128)(4,1)}), s8[4194304]{0:T(1024)(128)(4,1)S(1)}, s32[]{:S(2)}) async-start(s8[16777216]{0:T(1024)(128)(4,1)} %bitcast.102), calls=%async_computation.7 | async-start | bytes 8388608
  71.9 17.4 %slice-start.1 = ((s8[16777216]{0:T(1024)(128)(4,1)}), s8[4194304]{0:T(1024)(128)(4,1)S(1)}, s32[]{:S(2)}) async-start(s8[16777216]{0:T(1024)(128)(4,1)} %bitcast.102), calls=%async_computation.8 | async-start | bytes 8388608
  71.9 17.3 %slice-start.2 = ((s8[16777216]{0:T(1024)(128)(4,1)}), s8[4194304]{0:T(1024)(128)(4,1)S(1)}, s32[]{:S(2)}) async-start(s8[16777216]{0:T(1024)(128)(4,1)} %bitcast.102), calls=%async_computation.9 | async-start | bytes 8388608
  71.9 17.3 %slice-start.3 = ((s8[16777216]{0:T(1024)(128)(4,1)}), s8[4194304]{0:T(1024)(128)(4,1)S(1)}, s32[]{:S(2)}) async-start(s8[16777216]{0:T(1024)(128)(4,1)} %bitcast.102), calls=%async_computation.10 | async-start | bytes 8388608
  104.9 171.2 %all-reduce.9.cloned.1.call-start = ((), (), s32[]{:S(2)}) async-start(), calls=%async_computation.2 | async-start | bytes 4194304 | tf_op jit(solution)/shard_map/psum | solution.py:46
  225.3 127.0 %all-reduce.11.cloned.1.call-start = ((), (), s32[]{:S(2)}) async-start(), calls=%async_computation.3 | async-start | bytes 524288 | tf_op jit(solution)/shard_map/psum | solution.py:47
  281.1 204.7 %all-reduce.13.cloned.1.call-start = ((), (), s32[]{:S(2)}) async-start(), calls=%async_computation.4 | async-start | bytes 4194304 | tf_op jit(solution)/shard_map/psum | solution.py:43
  384.1 174.5 %all-reduce.15.cloned.1.call-start = ((), (), s32[]{:S(2)}) async-start(), calls=%async_computation.5 | async-start | bytes 4194304 | tf_op jit(solution)/shard_map/psum | solution.py:46
  488.6 1.3 copy-start.1
  507.8 127.0 %all-reduce.17.cloned.1.call-start = ((), (), s32[]{:S(2)}) async-start(), calls=%async_computation.6 | async-start | bytes 524288 | tf_op jit(solution)/shard_map/psum | solution.py:47
  642.3 2.0 copy-start.2
Sparse Core Ops, SparseCore 0:
  105.0 101.3 all-reduce.6
  225.5 50.6 all-reduce.8
  281.2 71.0 all-reduce.10
  384.2 101.5 all-reduce.12
  507.9 50.6 all-reduce.14
  563.6 71.0 all-reduce.16
